TPU v7x, 32 devices: a whole 2x2x4 slice. The times are simulated.
32 devices in a mesh: groups: 2 (over y), blk: 4 (over z), head: 4 (over x, core).
Axes of the slice: x: 2, y: 2, z: 4, core: 2. Of those that a mesh axis runs over, the one named last changes fastest.
Arguments:
- ctx_query: bfloat16 [4096, 8192], P(('groups', 'blk'), 'head'), parts along dimension 0, may hold values from -5 to 5
- ctx_key: bfloat16 [4096, 1024], P(('groups', 'blk'), 'head'), parts along dimension 0, may hold values from -5 to 5
- ctx_value: bfloat16 [4096, 1024], P(('groups', 'blk'), 'head'), parts along dimension 0, may hold values from -4.5 to 4.5
- opt_query: bfloat16 [128, 8192], P(('groups', 'blk'), 'head'), parts along dimension 0, may hold values from -5 to 5
- opt_owner: int32 [128], P('groups'), parts along dimension 0, may hold values from 0 to 3, as said below
- opt_slot: int32 [128], P('groups'), parts along dimension 0, may hold values from 0 to 31, as said below
- opt_length: int32 [128], P('groups'), parts along dimension 0, may hold values from 512 to 2048
Outputs:
- ctx_out: bfloat16 [4096, 8192], P(('groups', 'blk'), 'head'), parts along dimension 0
- opt_out: bfloat16 [256, 8192], P(('groups', 'blk'), 'head'), parts along dimension 0
There are 2 independent parts, one for each index of `groups`. A program takes and returns all parts, laid end to end along the dimension named above; each array names one. Nothing has to cross between parts.
Inputs may be any that keep to these rules, and one draw needn't show every extreme that they name: `opt_owner`: each option token has its own pair of owner block and slot; no block owns more than 32 option tokens, and one block owns exactly 32. `opt_slot`: slots of one owner are distinct.
All inputs are finite; a program needn't handle non-finite values.
Results may differ from a plain program's by a relative error of at most 0.017.
Values may be sent and summed in bfloat16 or wider, within the bound.
A program may use at most 64 MiB of HBM per device.

v0:
```python
import jax
import jax.numpy as jnp
from jax import lax
from jax.sharding import PartitionSpec as P

HD = 128
HQ = 64
KVH = 8
CAP = 32


def from_root(value, axis, root):
    mine = lax.axis_index(axis) == root
    return lax.psum(jnp.where(mine, value, jnp.zeros_like(value)), axis)


def soft_parts(query_head, keys, values, masks, scale):
    scores = []
    for key_part, mask_part in zip(keys, masks):
        raw = (
            jnp.einsum("td,sd->ts", query_head, key_part, preferred_element_type=jnp.float32)
            * scale
        )
        scores.append(jnp.where(mask_part, raw, -1e30))
    top = jnp.max(scores[0], axis=1)
    for extra in scores[1:]:
        top = jnp.maximum(top, jnp.max(extra, axis=1))
    total = jnp.zeros_like(top)
    accum = jnp.zeros((query_head.shape[0], values[0].shape[1]), jnp.float32)
    for score_part, value_part in zip(scores, values):
        expo = jnp.exp(score_part - top[:, None])
        total = total + jnp.sum(expo, axis=1)
        accum = accum + jnp.dot(
            expo.astype(jnp.bfloat16), value_part, preferred_element_type=jnp.float32
        )
    return (accum / total[:, None], top, total)


def body(ctx_query, ctx_key, ctx_value, opt_query, opt_owner, opt_slot, opt_length):
    group_size = HQ // KVH
    scale = HD ** (-0.5)
    block_index = lax.axis_index("blk")
    block_count = lax.axis_size("blk")
    rows = ctx_query.shape[0]
    local_heads = ctx_query.shape[1] // HD
    anchor_key, anchor_value = (from_root(ctx_key, "blk", 0), from_root(ctx_value, "blk", 0))
    spots = jnp.arange(rows, dtype=jnp.int32)
    causal = spots[:, None] >= spots[None, :]
    anchor_mask = jnp.broadcast_to(block_index > 0, (rows, rows))

    def phase_one(head_id, result):
        group = head_id // group_size
        query_head = lax.dynamic_slice_in_dim(ctx_query, head_id * HD, HD, 1)
        key_local = lax.dynamic_slice_in_dim(ctx_key, group * HD, HD, 1)
        value_local = lax.dynamic_slice_in_dim(ctx_value, group * HD, HD, 1)
        key_anchor = lax.dynamic_slice_in_dim(anchor_key, group * HD, HD, 1)
        value_anchor = lax.dynamic_slice_in_dim(anchor_value, group * HD, HD, 1)
        output, top, total = soft_parts(
            query_head,
            (key_anchor, key_local),
            (value_anchor, value_local),
            (anchor_mask, causal),
            scale,
        )
        return lax.dynamic_update_slice_in_dim(result, output.astype(jnp.bfloat16), head_id * HD, 1)

    ctx_out = lax.fori_loop(0, local_heads, phase_one, jnp.zeros(ctx_query.shape, jnp.bfloat16))
    all_queries = lax.all_gather(opt_query, "blk", axis=0, tiled=True)
    options = all_queries.shape[0]
    count = jnp.clip(opt_length - block_index * rows, 0, rows)
    live = count > 0
    visible = spots[None, :] < count[:, None]

    def phase_two(head_id, carry):
        partial_value, stats = carry
        group = head_id // group_size
        query_head = lax.dynamic_slice_in_dim(all_queries, head_id * HD, HD, 1)
        key_local = lax.dynamic_slice_in_dim(ctx_key, group * HD, HD, 1)
        value_local = lax.dynamic_slice_in_dim(ctx_value, group * HD, HD, 1)
        output, top, total = soft_parts(query_head, (key_local,), (value_local,), (visible,), scale)
        output = jnp.where(live[:, None], output, 0.0).astype(jnp.bfloat16)
        stat = jnp.where(live, top + jnp.log(total), -1e30)
        partial_value = lax.dynamic_update_slice_in_dim(partial_value, output, head_id * HD, 1)
        stats = lax.dynamic_update_slice_in_dim(stats, stat[:, None], head_id, 1)
        return (partial_value, stats)

    start = (
        jnp.zeros((options, local_heads * HD), jnp.bfloat16),
        jnp.zeros((options, local_heads), jnp.float32),
    )
    partial_value, stats = lax.fori_loop(0, local_heads, phase_two, start)
    slot_total = CAP * block_count
    where_to = opt_owner * CAP + opt_slot
    top_all = lax.pmax(stats, "blk")
    weight = jnp.exp(stats - top_all)
    weight_sum = lax.psum(weight, "blk")
    share = weight / weight_sum
    term = (
        partial_value.reshape(options, local_heads, HD).astype(jnp.float32) * share[:, :, None]
    ).reshape(options, local_heads * HD)
    buffer = jnp.zeros((slot_total, local_heads * HD), jnp.float32).at[where_to].set(term)
    opt_out = lax.psum_scatter(buffer.astype(jnp.bfloat16), "blk", scatter_dimension=0, tiled=True)
    return (ctx_out, opt_out)


def solution(mesh):
    return jax.shard_map(
        body,
        mesh=mesh,
        in_specs=(
            P(("groups", "blk"), "head"),
            P(("groups", "blk"), "head"),
            P(("groups", "blk"), "head"),
            P(("groups", "blk"), "head"),
            P("groups"),
            P("groups"),
            P("groups"),
        ),
        out_specs=(P(("groups", "blk"), "head"), P(("groups", "blk"), "head")),
        check_vma=False,
    )
```

profile of v0, /device:TPU:0, one launch (start us, length us, event | category | flops | bytes accessed | tf_op | source)
XLA Modules:
  0.0 127.9 jit_solution(5371850114910661687)
XLA Ops:
  7.2 1.9 %broadcast_select_fusion = (bf16[512,256]{1,0:T(8,128)(2,1)}, bf16[512,256]{1,0:T(8,128)(2,1)}) fusion(bf16[512,256]{1,0:T(8,128)(2,1)} %param.13, pred[]{:T(512)S(6)} %eq.4, bf16[512,256]{1,0:T(8,128)(2,1)} %param.12), kind=kLoop, calls=%fused_computation.54 | loop fusion | flops 262144 | bytes 1048577 | tf_op jit(solution)/shard_map/jit(_where)/select_n | solution.py:14
  9.2 15.8 %all_gather.3 = bf16[64,2048]{1,0:T(8,128)(2,1)S(1)} all-gather(bf16[16,2048]{1,0:T(8,128)(2,1)} %param.14), channel_id=1, replica_groups=mesh['groups'=2,'blk'=4,'head'=4] {'blk'}, dimensions={0}, use_global_device_ids=true | all-gather | bytes 327680 | tf_op jit(solution)/shard_map/all_gather | solution.py:68
  25.0 0.7 broadcast_compare_fusion
  25.7 12.9 %while.35 = (s32[]{:T(128)}, bf16[64,2048]{1,0:T(8,128)(2,1)S(1)}, f32[64,16]{0,1:T(8,128)S(1)}, pred[64]{0:T(512)(128)(4,1)S(1)}, bf16[64,2048]{1,0:T(8,128)(2,...) while((s32[]{:T(128)}, bf16[64,2048]{1,0:T(8,128)(2,1)S(1)}, ...), condition=%wide.region_11.12_spmd.clone, body=%wide.region_8.11_spmd.clone.sunk | while | flops 17063952 | bytes 692635 | solution.py:91
  38.6 11.7 %pmax.7 = f32[64,16]{0,1:T(8,128)S(1)} all-reduce(f32[64,16]{0,1:T(8,128)S(1)} %get-tuple-element.425), channel_id=1, replica_groups=mesh['groups'=2,'blk'=4,'head'=4] {'blk'}, use_global_device_ids=true, to_apply=%region_12.13 | all-reduce | flops 1024 | bytes 8192 | tf_op jit(solution)/shard_map/pmax | solution.py:94
  50.4 8.5 %psum.23 = f32[64,16]{0,1:T(8,128)S(1)} all-reduce(f32[64,16]{0,1:T(8,128)S(1)} %subtract_exponential_fusion.3), channel_id=1, replica_groups=mesh['groups'=2,'blk'=4,'head'=4] {'blk'}, use_global_device_ids=true, to_apply=%region_13.14 | all-reduce | flops 1024 | bytes 8192 | tf_op jit(solution)/shard_map/psum | solution.py:96
  59.2 1.3 %scatter_custom_fusion = f32[128,2048]{1,0:T(8,128)S(1)} fusion(s32[64]{0:T(128)S(1)} %compare_select_fusion, f32[8,8,16,128]{3,2,1,0:T(8,128)S(1)} %bitcast.8, bf16[64,2048]{1,0:T(8,128)(2,1)S(1)} %get-tuple-element.424, f32[]{:T(128)} %constant.275.clone.1), kind=kCustom, calls=%fused_computation.50 | custom fusion | flops 262144 | bytes 1835012 | tf_op jit(solution)/shard_map/scatter | solution.py:101
  60.6 0.9 convert_element_type.58
  61.8 0.6 copy-done.5
  62.5 57.1 %while.34 = (s32[]{:T(128)}, bf16[512,2048]{1,0:T(8,128)(2,1)S(1)}, bf16[512,2048]{1,0:T(8,128)(2,1)}, bf16[512,256]{1,0:T(8,128)(2,1)S(1)}, bf16[512,256]{1,0:T...) while((s32[]{:T(128)}, bf16[512,2048]{1,0:T(8,128)(2,1)S(1)}, ...), condition=%wide.region_7.8_spmd.clone, body=%wide.region_2.7_spmd.clone.sunk | while | flops 272563200 | bytes 7762787 | solution.py:67
  62.5 1.2 fusion.68
  63.8 1.2 fusion.69
  65.0 0.3 fusion.70
  65.7 0.4 fusion.72
  66.1 1.2 fusion.68
  67.3 1.2 fusion.69
  68.6 0.3 fusion.70
  69.2 0.4 fusion.72
  69.7 1.2 fusion.68
  70.9 1.2 fusion.69
  72.8 0.4 fusion.72
  73.3 1.2 fusion.68
  74.5 1.2 fusion.69
  76.4 0.4 fusion.72
  76.8 1.2 fusion.68
  78.1 1.2 fusion.69
  80.0 0.4 fusion.72
  80.4 1.2 fusion.68
  81.6 1.2 fusion.69
  83.5 0.4 fusion.72
  84.0 1.2 fusion.68
  85.2 1.2 fusion.69
  86.5 0.3 fusion.70
  87.1 0.4 fusion.72
  87.6 1.2 fusion.68
  88.8 1.2 fusion.69
  90.0 0.3 fusion.70
  90.7 0.4 fusion.72
  91.1 1.2 fusion.68
  92.4 1.2 fusion.69
  94.3 0.4 fusion.72
  94.7 1.2 fusion.68
  95.9 1.2 fusion.69
  97.8 0.4 fusion.72
  98.3 1.2 fusion.68
  99.5 1.2 fusion.69
  101.4 0.4 fusion.72
  101.9 1.2 fusion.68
  103.1 1.2 fusion.69
  105.0 0.4 fusion.72
  105.4 1.2 fusion.68
  106.7 1.2 fusion.69
  108.5 0.4 fusion.72
  109.0 1.2 fusion.68
  110.2 1.2 fusion.69
  111.5 0.3 fusion.70
  112.1 0.4 fusion.72
  112.6 1.2 fusion.68
  113.8 1.2 fusion.69
  115.7 0.4 fusion.72
  116.2 1.2 fusion.68
  117.4 1.2 fusion.69
  119.3 0.4 fusion.72
  119.7 1.3 %copy-done.1 = bf16[512,2048]{1,0:T(8,128)(2,1)} copy-done((bf16[512,2048]{1,0:T(8,128)(2,1)}, bf16[512,2048]{1,0:T(8,128)(2,1)S(1)}, u32[]{:S(2)}) %copy-start.1) | copy-done | bytes 2097176
  (167 shorter events, 21.8 us)
Async XLA Ops:
  7.2 18.5 %copy-start.4 = (bf16[512,256]{1,0:T(8,128)(2,1)S(1)}, bf16[512,256]{1,0:T(8,128)(2,1)}, u32[]{:S(2)}) copy-start(bf16[512,256]{1,0:T(8,128)(2,1)} %param.13) | copy-start | bytes 786436
  7.2 18.5 %copy-start = (bf16[512,256]{1,0:T(8,128)(2,1)S(1)}, bf16[512,256]{1,0:T(8,128)(2,1)}, u32[]{:S(2)}) copy-start(bf16[512,256]{1,0:T(8,128)(2,1)} %param.12) | copy-start | bytes 786436
  7.2 54.3 %all-reduce.3.cloned.1.call-start = ((), (), s32[]{:S(2)}) async-start(), calls=%async_computation.2 | async-start | bytes 1048576 | tf_op jit(solution)/shard_map/psum | solution.py:14
  9.2 110.5 %reduce-scatter.2.cloned.1.call-start = ((), (), s32[]{:S(2)}) async-start(), calls=%async_computation.1 | async-start | bytes 655360 | tf_op jit(solution)/shard_map/reduce_scatter | solution.py:102
  25.7 33.3 %copy-start.6 = (s32[64]{0:T(128)S(1)}, s32[64]{0:T(128)}, u32[]{:S(2)}) copy-start(s32[64]{0:T(128)} %param.16) | copy-start | bytes 772
  25.7 33.3 %copy-start.7 = (s32[64]{0:T(128)S(1)}, s32[64]{0:T(128)}, u32[]{:S(2)}) copy-start(s32[64]{0:T(128)} %param.15) | copy-start | bytes 772
  61.4 0.9 copy-start.5
  61.5 1.0 copy-start.2
  61.5 1.1 copy-start.3
  119.7 1.3 %copy-start.1 = (bf16[512,2048]{1,0:T(8,128)(2,1)}, bf16[512,2048]{1,0:T(8,128)(2,1)S(1)}, u32[]{:S(2)}) copy-start(bf16[512,2048]{1,0:T(8,128)(2,1)S(1)} %get-tuple-element.421) | copy-start | bytes 6291460
Sparse Core Ops, SparseCore 0:
  11.0 43.1 all-reduce.2
  61.6 21.6 reduce-scatter.1
where the time goes:
time: 129 us; the launch traced here: 128 us
  matrix products  59.5 us (46%)
  blocking collectives  36 us (28%)
  between operations  14.2 us (11%)
  other arithmetic  13 us (10%)
  local copies, waits for them, and re-layouts  3.26 us (3%)
  loops' own time  1.7 us (1%)
    dot_general x48, matrix products, soft_parts(): jnp.einsum('td,sd->ts', query_head, key_part, preferred_element_type=jnp....  43.5 us
    dot_general x48, matrix products, soft_parts(): jnp.dot(expo.astype(jnp.bfloat16), value_part, preferred_element_type=jnp...  15.9 us
    all_gather x1, blocking collectives, body(): all_queries = lax.all_gather(opt_query, 'blk', axis=0, tiled=True)  15.8 us
    pmax x1, blocking collectives, body(): top_all = lax.pmax(stats, 'blk')  11.7 us
    psum x1, blocking collectives, body(): weight_sum = lax.psum(weight, 'blk')  8.52 us
    reduce_sum x32, other arithmetic, soft_parts(): total = total + jnp.sum(expo, axis=1)  7.92 us
  transfers between devices with their start and end apart: 2, of which 0 were waited for; matrix products, arithmetic and copies ran while one was open for 56% of the time, Pallas kernels for 0%

commit v1 on v0

--- a/solution.py
+++ b/solution.py
@@ -2,6 +2,7 @@
 import jax.numpy as jnp
 from jax import lax
 from jax.sharding import PartitionSpec as P
+from jax.lax import axis_size, ppermute
 
 HD = 128
 HQ = 64
@@ -93,7 +94,17 @@
     where_to = opt_owner * CAP + opt_slot
     top_all = lax.pmax(stats, "blk")
     weight = jnp.exp(stats - top_all)
-    weight_sum = lax.psum(weight, "blk")
+
+    def assign_sizes(local_array):
+        n_shards = axis_size("blk")
+        last = local_array
+        for rr in [d for d in (1, 2, 4, 8, 16) if d < n_shards]:
+            last = last + ppermute(
+                last, axis_name="blk", perm=[(u, u ^ rr) for u in range(n_shards)]
+            )
+        return last
+
+    weight_sum = assign_sizes(weight)
     share = weight / weight_sum
     term = (
         partial_value.reshape(options, local_heads, HD).astype(jnp.float32) * share[:, :, None]

time: 129 us -> 129 us (level)
  blocking collectives: 36 us -> 27.8 us
  waiting for transfers between devices: 0.07 us -> 8.22 us
    psum x1 -> x0, blocking collectives: 8.52 us -> none  [body(): weight_sum = lax.psum(weight, 'blk')]
    ppermute x0 -> x2, waiting for transfers between devices: none -> 8.15 us  [assign_sizes(): ppermute(last, axis_name='blk', perm=[(u, u ^ rr) for u in range(n_shards)])]
  transfers between devices with their start and end apart: 2 -> 4, of which waited for: 0 -> 2; matrix products, arithmetic and copies ran while one was open for 56% -> 56% of each run, Pallas kernels for 0% -> 0%
where the time goes in v1:
time: 129 us; the launch traced here: 128 us
  matrix products  59.5 us (46%)
  blocking collectives  27.8 us (22%)
  between operations  14.2 us (11%)
  other arithmetic  13 us (10%)
  waiting for transfers between devices  8.22 us (6%)
  local copies, waits for them, and re-layouts  3.26 us (3%)
  loops' own time  1.71 us (1%)
    dot_general x48, matrix products, soft_parts(): jnp.einsum('td,sd->ts', query_head, key_part, preferred_element_type=jnp....  43.6 us
    dot_general x48, matrix products, soft_parts(): jnp.dot(expo.astype(jnp.bfloat16), value_part, preferred_element_type=jnp...  15.9 us
    all_gather x1, blocking collectives, body(): all_queries = lax.all_gather(opt_query, 'blk', axis=0, tiled=True)  15.8 us
    pmax x1, blocking collectives, body(): top_all = lax.pmax(stats, 'blk')  12 us
    ppermute x2, waiting for transfers between devices, assign_sizes(): ppermute(last, axis_name='blk', perm=[(u, u ^ rr) for u in range(n_shards)])  8.15 us
    reduce_sum x32, other arithmetic, soft_parts(): total = total + jnp.sum(expo, axis=1)  7.92 us
  transfers between devices with their start and end apart: 4, of which 2 were waited for; matrix products, arithmetic and copies ran while one was open for 56% of the time, Pallas kernels for 0%

profile of v1, /device:TPU:0, one launch (start us, length us, event | category | flops | bytes accessed | tf_op | source)
XLA Modules:
  0.0 127.9 jit_solution(10184053113526831672)
XLA Ops:
  7.2 1.9 %broadcast_select_fusion = (bf16[512,256]{1,0:T(8,128)(2,1)}, bf16[512,256]{1,0:T(8,128)(2,1)}) fusion(bf16[512,256]{1,0:T(8,128)(2,1)} %param.13, pred[]{:T(512)S(6)} %eq.4, bf16[512,256]{1,0:T(8,128)(2,1)} %param.12), kind=kLoop, calls=%fused_computation.54 | loop fusion | flops 262144 | bytes 1048577 | tf_op jit(solution)/shard_map/jit(_where)/select_n | solution.py:15
  9.2 15.8 %all_gather.3 = bf16[64,2048]{1,0:T(8,128)(2,1)S(1)} all-gather(bf16[16,2048]{1,0:T(8,128)(2,1)} %param.14), channel_id=1, replica_groups=mesh['groups'=2,'blk'=4,'head'=4] {'blk'}, dimensions={0}, use_global_device_ids=true | all-gather | bytes 327680 | tf_op jit(solution)/shard_map/all_gather | solution.py:69
  25.0 0.7 broadcast_compare_fusion
  25.7 12.9 %while.35 = (s32[]{:T(128)}, bf16[64,2048]{1,0:T(8,128)(2,1)S(1)}, f32[64,16]{0,1:T(8,128)S(1)}, pred[64]{0:T(512)(128)(4,1)S(1)}, bf16[64,2048]{1,0:T(8,128)(2,...) while((s32[]{:T(128)}, bf16[64,2048]{1,0:T(8,128)(2,1)S(1)}, ...), condition=%wide.region_11.12_spmd.clone, body=%wide.region_8.11_spmd.clone.sunk | while | flops 17063952 | bytes 692635 | solution.py:92
  38.6 12.0 %pmax.7 = f32[64,16]{0,1:T(8,128)S(1)} all-reduce(f32[64,16]{0,1:T(8,128)S(1)} %get-tuple-element.425), channel_id=1, replica_groups=mesh['groups'=2,'blk'=4,'head'=4] {'blk'}, use_global_device_ids=true, to_apply=%region_12.13 | all-reduce | flops 1024 | bytes 8192 | tf_op jit(solution)/shard_map/pmax | solution.py:95
  50.8 3.6 %collective-permute-done = f32[64,16]{0,1:T(8,128)S(1)} collective-permute-done((f32[64,16]{0,1:T(8,128)S(1)}, f32[64,16]{0,1:T(8,128)S(1)}, u32[]{:S(2)}, u32[]{:S(2)}) %collective-permute-start) | collective-permute-done | bytes 4128 | tf_op jit(solution)/shard_map/ppermute | solution.py:102
  54.4 4.5 %collective-permute-done.1 = f32[64,16]{0,1:T(8,128)S(1)} collective-permute-done((f32[64,16]{0,1:T(8,128)S(1)}, f32[64,16]{0,1:T(8,128)S(1)}, u32[]{:S(2)}, u32[]{:S(2)}) %collective-permute-start.1) | collective-permute-done | bytes 4128 | tf_op jit(solution)/shard_map/ppermute | solution.py:102
  59.2 1.3 %scatter_custom_fusion = f32[128,2048]{1,0:T(8,128)S(1)} fusion(s32[64]{0:T(128)S(1)} %compare_select_fusion, f32[8,8,16,128]{3,2,1,0:T(8,128)S(1)} %bitcast.8, bf16[64,2048]{1,0:T(8,128)(2,1)S(1)} %get-tuple-element.424, f32[]{:T(128)} %constant.275.clone.1), kind=kCustom, calls=%fused_computation.50 | custom fusion | flops 262144 | bytes 1835012 | tf_op jit(solution)/shard_map/scatter | solution.py:112
  60.6 0.9 convert_element_type.58
  61.8 0.6 copy-done.5
  62.6 57.1 %while.34 = (s32[]{:T(128)}, bf16[512,2048]{1,0:T(8,128)(2,1)S(1)}, bf16[512,2048]{1,0:T(8,128)(2,1)}, bf16[512,256]{1,0:T(8,128)(2,1)S(1)}, bf16[512,256]{1,0:T...) while((s32[]{:T(128)}, bf16[512,2048]{1,0:T(8,128)(2,1)S(1)}, ...), condition=%wide.region_7.8_spmd.clone, body=%wide.region_2.7_spmd.clone.sunk | while | flops 272563200 | bytes 7762787 | solution.py:68
  62.6 1.2 fusion.68
  63.8 1.2 fusion.69
  65.7 0.4 fusion.72
  66.1 1.2 fusion.68
  67.4 1.2 fusion.69
  68.6 0.3 fusion.70
  69.3 0.4 fusion.72
  69.7 1.2 fusion.68
  70.9 1.2 fusion.69
  72.8 0.4 fusion.72
  73.3 1.2 fusion.68
  74.5 1.2 fusion.69
  76.4 0.4 fusion.72
  76.9 1.2 fusion.68
  78.1 1.2 fusion.69
  80.0 0.4 fusion.72
  80.4 1.2 fusion.68
  81.7 1.2 fusion.69
  82.9 0.3 fusion.70
  83.6 0.4 fusion.72
  84.0 1.2 fusion.68
  85.2 1.2 fusion.69
  87.1 0.4 fusion.72
  87.6 1.2 fusion.68
  88.8 1.2 fusion.69
  90.1 0.3 fusion.70
  90.7 0.4 fusion.72
  91.2 1.2 fusion.68
  92.4 1.2 fusion.69
  94.3 0.4 fusion.72
  94.7 1.2 fusion.68
  96.0 1.2 fusion.69
  97.8 0.4 fusion.72
  98.3 1.2 fusion.68
  99.5 1.2 fusion.69
  101.4 0.4 fusion.72
  101.9 1.2 fusion.68
  103.1 1.2 fusion.69
  105.0 0.4 fusion.72
  105.5 1.2 fusion.68
  106.7 1.2 fusion.69
  108.6 0.4 fusion.72
  109.0 1.2 fusion.68
  110.2 1.2 fusion.69
  111.5 0.3 fusion.70
  112.1 0.4 fusion.72
  112.6 1.2 fusion.68
  113.8 1.2 fusion.69
  115.7 0.4 fusion.72
  116.2 1.2 fusion.68
  117.4 1.2 fusion.69
  119.3 0.4 fusion.72
  119.8 1.3 %copy-done.1 = bf16[512,2048]{1,0:T(8,128)(2,1)} copy-done((bf16[512,2048]{1,0:T(8,128)(2,1)}, bf16[512,2048]{1,0:T(8,128)(2,1)S(1)}, u32[]{:S(2)}) %copy-start.1) | copy-done | bytes 2097176
  (171 shorter events, 22.2 us)
Async XLA Ops:
  7.2 18.5 %copy-start.4 = (bf16[512,256]{1,0:T(8,128)(2,1)S(1)}, bf16[512,256]{1,0:T(8,128)(2,1)}, u32[]{:S(2)}) copy-start(bf16[512,256]{1,0:T(8,128)(2,1)} %param.13) | copy-start | bytes 786436
  7.2 18.5 %copy-start = (bf16[512,256]{1,0:T(8,128)(2,1)S(1)}, bf16[512,256]{1,0:T(8,128)(2,1)}, u32[]{:S(2)}) copy-start(bf16[512,256]{1,0:T(8,128)(2,1)} %param.12) | copy-start | bytes 786436
  7.2 54.3 %all-reduce.3.cloned.1.call-start = ((), (), s32[]{:S(2)}) async-start(), calls=%async_computation.2 | async-start | bytes 1048576 | tf_op jit(solution)/shard_map/psum | solution.py:15
  9.2 110.6 %reduce-scatter.2.cloned.1.call-start = ((), (), s32[]{:S(2)}) async-start(), calls=%async_computation.1 | async-start | bytes 655360 | tf_op jit(solution)/shard_map/reduce_scatter | solution.py:113
  25.7 28.7 %copy-start.6 = (s32[64]{0:T(128)S(1)}, s32[64]{0:T(128)}, u32[]{:S(2)}) copy-start(s32[64]{0:T(128)} %param.16) | copy-start | bytes 772
  25.7 28.7 %copy-start.7 = (s32[64]{0:T(128)S(1)}, s32[64]{0:T(128)}, u32[]{:S(2)}) copy-start(s32[64]{0:T(128)} %param.15) | copy-start | bytes 772
  50.7 3.7 %collective-permute-start = (f32[64,16]{0,1:T(8,128)S(1)}, f32[64,16]{0,1:T(8,128)S(1)}, u32[]{:S(2)}, u32[]{:S(2)}) collective-permute-start(f32[64,16]{0,1:T(8,128)S(1)} %subtract_exponential_fusion.3), channel_id=1, source_target_pairs={{0,4},{4,0},{8,12},{12,8},{1,5},{5,1},{9,13},{13,9},{2,6},{6,2},{1... | collective-permute-start | bytes 12296 | tf_op jit(solution)/shard_map/ppermute | solution.py:102
  54.4 4.5 %collective-permute-start.1 = (f32[64,16]{0,1:T(8,128)S(1)}, f32[64,16]{0,1:T(8,128)S(1)}, u32[]{:S(2)}, u32[]{:S(2)}) collective-permute-start(f32[64,16]{0,1:T(8,128)S(1)} %add.172), channel_id=1, source_target_pairs={{0,8},{4,12},{8,0},{12,4},{1,9},{5,13},{9,1},{13,5},{2,10},{6,14},... | collective-permute-start | bytes 12296 | tf_op jit(solution)/shard_map/ppermute | solution.py:102
  61.4 0.9 copy-start.5
  61.5 1.0 copy-start.2
  61.5 1.1 copy-start.3
  119.7 1.3 %copy-start.1 = (bf16[512,2048]{1,0:T(8,128)(2,1)}, bf16[512,2048]{1,0:T(8,128)(2,1)S(1)}, u32[]{:S(2)}) copy-start(bf16[512,2048]{1,0:T(8,128)(2,1)S(1)} %get-tuple-element.421) | copy-start | bytes 6291460
Sparse Core Ops, SparseCore 0:
  11.0 42.9 all-reduce.2
  61.6 19.8 reduce-scatter.1
